TPU v7x, 256 devices: a whole 4x4x8 slice. The times are simulated.
256 devices in a mesh: gx: 4 (over z_lo), gy: 4 (over x), gz: 16 (over y, z_hi, core).
Axes of the slice: x: 4, y: 4, z: 8 (z_hi: 2, z_lo: 4; z = z_hi * 4 + z_lo), core: 2. Of those that a mesh axis runs over, the one named last changes fastest.
Arguments:
- features: bfloat16 [8, 16, 16, 128, 256], P('gx', 'gy', 'gz'), may hold values from -6 to 6
- fractions: bfloat16 [8, 16, 16, 3, 128], P('gx', 'gy', 'gz'), may hold values from 0 to 0.98828125
- occupied: int32 [8, 16, 16, 128], P('gx', 'gy', 'gz'), may hold values 0 or 1
- wave_index: int32 [3, 512], replicated, may hold values from -14 to 14, as said below
- radial_weight: float32 [8, 4], replicated, may hold values from -4 to 4
- ewald_mix: float32 [256, 256], replicated, may hold values from -0.375 to 0.375
- msg_weight: bfloat16 [256, 256], replicated, may hold values from -0.375 to 0.375
- ewald_weight: bfloat16 [256, 256], replicated, may hold values from -0.375 to 0.375
- out_weight: bfloat16 [256, 256], replicated, may hold values from -0.375 to 0.375
Outputs:
- updated: bfloat16 [8, 16, 16, 128, 256], P('gx', 'gy', 'gz')
Inputs may be any that keep to these rules, and one draw needn't show every extreme that they name: `wave_index`: no wavevector is zero, and no two wavevectors are equal or opposite.
All inputs are finite; a program needn't handle non-finite values. No bound on the sum of `occupied` on one device may be relied on, other than what follows from the above.
Results may differ from a plain program's by a relative error of at most 0.007.
Values may be sent and summed in bfloat16 or wider, within the bound.
No kernel may reach another device: no remote copies, remote signals or barrier semaphores. Data moves between devices by JAX's collectives and lax.ppermute only.
A program may use at most 64 MiB of HBM per device.

v0:
```python
import math

import jax
import jax.numpy as jnp
from jax import lax
from jax.sharding import PartitionSpec as P

sharpness = 16.0
smearing = 0.04
screening = 4.0
strength = 24.0


def padded(x, sides, width):
    for axis, dim in sides:
        count, length = (lax.axis_size(axis), x.shape[dim])
        up = [(i, (i + 1) % count) for i in range(count)]
        down = [(j, i) for i, j in up]
        last = lax.slice_in_dim(x, length - width, length, axis=dim)
        first = lax.slice_in_dim(x, 0, width, axis=dim)
        before = lax.ppermute(last, axis, up)
        after = lax.ppermute(first, axis, down)
        x = jnp.concatenate([before, x, after], axis=dim)
    return x


def pair_weights(home_geom, near_geom, shift_vec, radial_weight, self_pair):
    slot_count = home_geom.shape[2]
    dist_sq = jnp.zeros((home_geom.shape[0], slot_count, slot_count), jnp.float32)
    for axis_id in range(3):
        axis_gap = (
            near_geom[:, axis_id, None, :] + shift_vec[axis_id] - home_geom[:, axis_id, :, None]
        )
        dist_sq = dist_sq + axis_gap * axis_gap
    distance = jnp.sqrt(dist_sq)
    envelope = jnp.square(jnp.maximum(1.0 - dist_sq, 0.0)) * near_geom[:, 3, None, :]
    envelope = envelope * (1.0 - self_pair * jnp.eye(slot_count, dtype=jnp.float32))
    level_count = radial_weight.shape[0]
    radial_sum = jnp.zeros(
        (home_geom.shape[0], radial_weight.shape[1], slot_count, slot_count), jnp.float32
    )
    for level_id in range(level_count):
        radial_bump = jnp.exp(-sharpness * jnp.square(distance - level_id / (level_count - 1)))
        radial_sum = (
            radial_sum + radial_bump[:, None] * radial_weight[level_id][None, :, None, None]
        )
    return (radial_sum * envelope[:, None]).astype(jnp.bfloat16)


def body(
    features,
    fractions,
    occupied,
    wave_index,
    radial_weight,
    ewald_mix,
    msg_weight,
    ewald_weight,
    out_weight,
):
    cells_x, cells_y, cells_z, slot_count, feat_width = features.shape
    head_count = radial_weight.shape[1]
    head_width = feat_width // head_count
    cell_count = cells_x * cells_y * cells_z
    atom_rows = cell_count * slot_count
    geometry = jnp.concatenate([fractions, occupied[:, :, :, None, :].astype(jnp.bfloat16)], axis=3)
    wide_feat = padded(features, (("gx", 0), ("gy", 1), ("gz", 2)), 1)
    wide_geom = padded(geometry, (("gx", 0), ("gy", 1), ("gz", 2)), 1)
    home_geom = geometry.reshape(cell_count, 4, slot_count).astype(jnp.float32)
    anchor = jnp.int32(0)

    def add_offset(offset_id, msg_sum):
        step_x = offset_id // 9 - 1
        step_y = offset_id // 3 % 3 - 1
        step_z = offset_id % 3 - 1
        near_feat = lax.dynamic_slice(
            wide_feat,
            (step_x + 1, step_y + 1, step_z + 1, anchor, anchor),
            (cells_x, cells_y, cells_z, slot_count, feat_width),
        )
        near_feat = near_feat.reshape(cell_count, slot_count, head_count, head_width)
        near_geom = lax.dynamic_slice(
            wide_geom,
            (step_x + 1, step_y + 1, step_z + 1, anchor, anchor),
            (cells_x, cells_y, cells_z, 4, slot_count),
        )
        near_geom = near_geom.reshape(cell_count, 4, slot_count).astype(jnp.float32)
        shift_vec = jnp.stack([step_x, step_y, step_z]).astype(jnp.float32)
        self_pair = (offset_id == 13).astype(jnp.float32)
        weights = pair_weights(home_geom, near_geom, shift_vec, radial_weight, self_pair)
        return msg_sum + jnp.einsum(
            "nhpq,nqhc->nphc", weights, near_feat, preferred_element_type=jnp.float32
        )

    msg_sum = lax.fori_loop(
        0, 27, add_offset, jnp.zeros((cell_count, slot_count, head_count, head_width), jnp.float32)
    )
    scaled = msg_sum.reshape(cell_count, slot_count, feat_width) * (
        1.0 / math.sqrt(4.0 * slot_count)
    )
    messages = scaled.astype(jnp.bfloat16).reshape(atom_rows, feat_width)
    grid_x = lax.axis_size("gx") * cells_x
    grid_y = lax.axis_size("gy") * cells_y
    grid_z = lax.axis_size("gz") * cells_z
    devices = lax.axis_size("gx") * lax.axis_size("gy") * lax.axis_size("gz")
    wave_count = wave_index.shape[1]
    lengths = jnp.array([grid_x, grid_y, grid_z], jnp.float32)
    wave_vec = 2.0 * math.pi * wave_index.astype(jnp.float32) / lengths[:, None]
    wave_sq = jnp.sum(wave_vec * wave_vec, axis=0)
    damping = (
        strength
        * jnp.exp(-0.5 * smearing * wave_sq)
        / (wave_sq + screening)
        * (1.0 / math.sqrt(atom_rows * devices * wave_count))
    )
    start_x = (lax.axis_index("gx") * cells_x + jnp.arange(cells_x, dtype=jnp.int32)).astype(
        jnp.float32
    )[:, None, None, None]
    start_y = (lax.axis_index("gy") * cells_y + jnp.arange(cells_y, dtype=jnp.int32)).astype(
        jnp.float32
    )[None, :, None, None]
    start_z = (lax.axis_index("gz") * cells_z + jnp.arange(cells_z, dtype=jnp.int32)).astype(
        jnp.float32
    )[None, None, :, None]
    local_frac = fractions.astype(jnp.float32)
    pos_x = start_x + local_frac[:, :, :, 0]
    pos_y = start_y + local_frac[:, :, :, 1]
    pos_z = start_z + local_frac[:, :, :, 2]
    phase_rows = (
        pos_x[..., None] * wave_vec[0]
        + pos_y[..., None] * wave_vec[1]
        + pos_z[..., None] * wave_vec[2]
    )
    phase_rows = phase_rows.reshape(atom_rows, wave_count)
    wave_basis = jnp.concatenate([jnp.cos(phase_rows), jnp.sin(phase_rows)], axis=1).astype(
        jnp.bfloat16
    )
    masked = (features * occupied[..., None].astype(jnp.bfloat16)).reshape(atom_rows, feat_width)
    partial_value = lax.dot_general(
        wave_basis, masked, (((0,), (0,)), ((), ())), preferred_element_type=jnp.float32
    )
    partial_value = partial_value.reshape(2, wave_count, feat_width)
    wave_sums = lax.psum(partial_value, ("gx", "gy", "gz"))
    mixed_rows = jnp.dot(
        wave_sums.reshape(2 * wave_count, feat_width), ewald_mix, precision=lax.Precision.HIGHEST
    )
    mixed_rows = mixed_rows.reshape(2, wave_count, feat_width)
    filtered = (mixed_rows * damping[None, :, None]).astype(jnp.bfloat16)
    values = jnp.dot(
        wave_basis, filtered.reshape(2 * wave_count, feat_width), preferred_element_type=jnp.float32
    )
    ewald_out = values.astype(jnp.bfloat16)
    joined = jnp.dot(messages, msg_weight, preferred_element_type=jnp.float32) + jnp.dot(
        ewald_out, ewald_weight, preferred_element_type=jnp.float32
    )
    hidden = jax.nn.silu(joined).astype(jnp.bfloat16)
    result = features.reshape(atom_rows, feat_width).astype(jnp.float32) + jnp.dot(
        hidden, out_weight, preferred_element_type=jnp.float32
    )
    result = result * occupied.reshape(atom_rows, 1).astype(jnp.float32)
    return result.astype(jnp.bfloat16).reshape(features.shape)


def solution(mesh):
    in_specs = (
        P("gx", "gy", "gz", None, None),
        P("gx", "gy", "gz", None, None),
        P("gx", "gy", "gz", None),
        P(),
        P(),
        P(),
        P(),
        P(),
        P(),
    )
    out_specs = P("gx", "gy", "gz", None, None)
    return jax.shard_map(body, mesh=mesh, in_specs=in_specs, out_specs=out_specs, check_vma=False)
```

profile of v0, /device:TPU:2, one launch (start us, length us, event | category | flops | bytes accessed | tf_op | source)
XLA Modules:
  0.0 642.4 jit_solution(9146714887031135012)
XLA Ops:
  17.0 8.9 %cosine_convert_fusion = (bf16[1024,512]{1,0:T(8,128)(2,1)S(1)}, bf16[1024,512]{1,0:T(8,128)(2,1)S(1)}) fusion(f32[512]{0:T(512)S(1)} %bitcast.132, f32[1024]{0:T(1024)S(1)} %bitcast.126, f32[512]{0:T(512)S(1)} %bitcast.133, f32[1024]{0:T(1024)S(1)} %add.807, f32[512]{0:T(512)S(1)} %bitcast.131, f32[1024]{0:T(1024)S(1)} %add.802), kind=kLoop, calls=%fused_computation.57 | loop fusion | flops 3670016 | bytes 2115584 | tf_op jit(solution)/shard_map/convert.2
  38.4 7.8 %collective-permute-start.5 = (bf16[4,6,1,128,256]{3,4,1,0,2:T(8,128)(2,1)}, bf16[4,6,1,128,256]{3,4,1,0,2:T(8,128)(2,1)}, u32[]{:S(2)}, u32[]{:S(2)}) collective-permute-start(bf16[4,6,1,128,256]{3,4,1,0,2:T(8,128)(2,1)} %pad_maximum_fusion.2), channel_id=1, source_target_pairs={{1,0},{2,1},{3,2},{4,3},{5,4},{6,5},{7,6},{8,7},{9,8},{10,9},{11,1... | collective-permute-start | bytes 4718600 | tf_op jit(solution)/shard_map/ppermute | solution.py:22
  53.0 7.8 %collective-permute-start.11 = (bf16[4,6,1,4,128]{4,1,0,3,2:T(8,128)(2,1)S(1)}, bf16[4,6,1,4,128]{4,1,0,3,2:T(8,128)(2,1)S(1)}, u32[]{:S(2)}, u32[]{:S(2)}) collective-permute-start(bf16[4,6,1,4,128]{4,1,0,3,2:T(8,128)(2,1)S(1)} %pad_maximum_fusion.14), channel_id=1, source_target_pairs={{1,0},{2,1},{3,2},{4,3},{5,4},{6,5},{7,6},{8,7},{9,8},{10,9},{11,1... | collective-permute-start | bytes 73736 | tf_op jit(solution)/shard_map/ppermute | solution.py:22
  60.8 54.6 %collective-permute-done.10 = bf16[4,6,1,4,128]{4,1,0,3,2:T(8,128)(2,1)S(1)} collective-permute-done((bf16[4,6,1,4,128]{4,1,0,3,2:T(8,128)(2,1)S(1)}, bf16[4,6,1,4,128]{4,1,0,3,2:T(8,128)(2,1)S(1)}, u32[]{:S(2)}, u32[]{:S(2)}) %collective-permute-start.10) | collective-permute-done | bytes 24608 | tf_op jit(solution)/shard_map/ppermute | solution.py:21
  115.4 210.6 %all-reduce.2.cloned.1.call-done = f32[2,512,256]{2,1,0:T(8,128)} async-done(((f32[2,512,256]{2,1,0:T(8,128)}), f32[2,512,256]{2,1,0:T(8,128)}) %all-reduce.2.cloned.1.call-update) | async-done | bytes 1048592 | tf_op jit(solution)/shard_map/psum | solution.py:143
  329.1 5.1 pad_maximum_fusion
  334.2 294.5 %while.19 = (s32[]{:T(128)}, f32[8,128,4,64]{1,3,2,0:T(8,128)}, bf16[4,6,3,128,256]{3,4,1,0,2:T(8,128)(2,1)}, bf16[4,6,3,4,128]{4,1,0,3,2:T(8,128)(2,1)S(1)}, f3...) while((s32[]{:T(128)}, f32[8,128,4,64]{1,3,2,0:T(8,128)}, ...), condition=%wide.region_1.2_spmd.clone, body=%wide.region_0.1_spmd.clone.sunk | while | flops 81321008 | bytes 13366249 | solution.py:95
  362.3 4.3 fusion.62
  373.2 4.3 fusion.62
  384.1 4.3 fusion.62
  395.0 4.3 fusion.62
  406.0 4.3 fusion.62
  427.8 4.3 fusion.62
  438.7 4.3 fusion.62
  449.6 4.3 fusion.62
  482.4 4.3 fusion.62
  493.3 4.3 fusion.62
  504.2 4.3 fusion.62
  537.0 4.3 fusion.62
  547.9 4.3 fusion.62
  558.8 4.3 fusion.62
  591.6 4.3 fusion.62
  602.5 4.3 fusion.62
  613.4 4.3 fusion.62
  (351 shorter events, 259.0 us)
Async XLA Ops:
  6.5 319.5 %copy-start = (f32[256,256]{1,0:T(8,128)S(1)}, f32[256,256]{1,0:T(8,128)}, u32[]{:S(2)}) copy-start(f32[256,256]{1,0:T(8,128)} %param.17) | copy-start | bytes 786436
  6.5 10.2 %copy-start.17 = (f32[3]{0:T(128)S(1)}, f32[3]{0:T(128)}, u32[]{:S(2)}) copy-start(f32[3]{0:T(128)} %constant.269) | copy-start | bytes 40
  6.5 6.2 copy-start.14
  6.5 6.3 copy-start.11
  6.5 10.2 %copy-start.15 = (s32[3,512]{1,0:T(4,128)S(1)}, s32[3,512]{1,0:T(4,128)}, u32[]{:S(2)}) copy-start(s32[3,512]{1,0:T(4,128)} %param.15) | copy-start | bytes 18436
  6.5 319.5 %all-reduce.2.cloned.1.call-start = ((), (), s32[]{:S(2)}) async-start(), calls=%async_computation | async-start | bytes 2097152 | tf_op jit(solution)/shard_map/psum | solution.py:143
  8.0 18.0 %collective-permute-start = (bf16[1,4,1,128,256]{3,4,1,0,2:T(8,128)(2,1)S(1)}, bf16[1,4,1,128,256]{3,4,1,0,2:T(8,128)(2,1)S(1)}, u32[]{:S(2)}, u32[]{:S(2)}) collective-permute-start(bf16[1,4,1,128,256]{3,4,1,0,2:T(8,128)(2,1)S(1)} %get-tuple-element.358), channel_id=1, source_target_pairs={{0,64},{64,128},{128,192},{192,0},{1,65},{65,129},{129,193},{193,1... | collective-permute-start | bytes 786440 | tf_op jit(solution)/shard_map/ppermute | solution.py:21
  10.0 16.0 %collective-permute-start.1 = (bf16[1,4,1,128,256]{3,4,1,0,2:T(8,128)(2,1)S(1)}, bf16[1,4,1,128,256]{3,4,1,0,2:T(8,128)(2,1)S(1)}, u32[]{:S(2)}, u32[]{:S(2)}) collective-permute-start(bf16[1,4,1,128,256]{3,4,1,0,2:T(8,128)(2,1)S(1)} %get-tuple-element.359), channel_id=1, source_target_pairs={{64,0},{128,64},{192,128},{0,192},{65,1},{129,65},{193,129},{1,193... | collective-permute-start | bytes 786440 | tf_op jit(solution)/shard_map/ppermute | solution.py:22
  12.8 35.0 %collective-permute-start.6 = (bf16[1,4,1,4,128]{4,1,0,3,2:T(4,128)(2,1)S(1)}, bf16[1,4,1,4,128]{4,1,0,3,2:T(4,128)(2,1)S(1)}, u32[]{:S(2)}, u32[]{:S(2)}) collective-permute-start(bf16[1,4,1,4,128]{4,1,0,3,2:T(4,128)(2,1)S(1)} %get-tuple-element.367), channel_id=1, source_target_pairs={{0,64},{64,128},{128,192},{192,0},{1,65},{65,129},{129,193},{193,1... | collective-permute-start | bytes 12296 | tf_op jit(solution)/shard_map/ppermute | solution.py:21
  12.9 35.0 %collective-permute-start.7 = (bf16[1,4,1,4,128]{4,1,0,3,2:T(4,128)(2,1)S(1)}, bf16[1,4,1,4,128]{4,1,0,3,2:T(4,128)(2,1)S(1)}, u32[]{:S(2)}, u32[]{:S(2)}) collective-permute-start(bf16[1,4,1,4,128]{4,1,0,3,2:T(4,128)(2,1)S(1)} %get-tuple-element.368), channel_id=1, source_target_pairs={{64,0},{128,64},{192,128},{0,192},{65,1},{129,65},{193,129},{1,193... | collective-permute-start | bytes 12296 | tf_op jit(solution)/shard_map/ppermute | solution.py:22
  26.0 3.1 copy-start.3
  27.0 7.5 %collective-permute-start.2 = (bf16[4,1,1,128,256]{3,4,1,0,2:T(8,128)(2,1)}, bf16[4,1,1,128,256]{3,4,1,0,2:T(8,128)(2,1)}, u32[]{:S(2)}, u32[]{:S(2)}) collective-permute-start(bf16[4,1,1,128,256]{3,4,1,0,2:T(8,128)(2,1)} %get-tuple-element.356), channel_id=1, source_target_pairs={{0,16},{16,32},{32,48},{48,0},{1,17},{17,33},{33,49},{49,1},{2,18}... | collective-permute-start | bytes 786440 | tf_op jit(solution)/shard_map/ppermute | solution.py:21
  28.5 7.2 %collective-permute-start.3 = (bf16[4,1,1,128,256]{3,4,1,0,2:T(8,128)(2,1)}, bf16[4,1,1,128,256]{3,4,1,0,2:T(8,128)(2,1)}, u32[]{:S(2)}, u32[]{:S(2)}) collective-permute-start(bf16[4,1,1,128,256]{3,4,1,0,2:T(8,128)(2,1)} %get-tuple-element.357), channel_id=1, source_target_pairs={{16,0},{32,16},{48,32},{0,48},{17,1},{33,17},{49,33},{1,49},{18,2}... | collective-permute-start | bytes 786440 | tf_op jit(solution)/shard_map/ppermute | solution.py:22
  38.4 290.7 %collective-permute-start.4 = (bf16[4,6,1,128,256]{3,4,1,0,2:T(8,128)(2,1)}, bf16[4,6,1,128,256]{3,4,1,0,2:T(8,128)(2,1)}, u32[]{:S(2)}, u32[]{:S(2)}) collective-permute-start(bf16[4,6,1,128,256]{3,4,1,0,2:T(8,128)(2,1)} %pad_maximum_fusion.2), channel_id=1, source_target_pairs={{0,1},{1,2},{2,3},{3,4},{4,5},{5,6},{6,7},{7,8},{8,9},{9,10},{10,1... | collective-permute-start | bytes 4718600 | tf_op jit(solution)/shard_map/ppermute | solution.py:21
  38.4 290.7 %collective-permute-start.5 = (bf16[4,6,1,128,256]{3,4,1,0,2:T(8,128)(2,1)}, bf16[4,6,1,128,256]{3,4,1,0,2:T(8,128)(2,1)}, u32[]{:S(2)}, u32[]{:S(2)}) collective-permute-start(bf16[4,6,1,128,256]{3,4,1,0,2:T(8,128)(2,1)} %pad_maximum_fusion.2), channel_id=1, source_target_pairs={{1,0},{2,1},{3,2},{4,3},{5,4},{6,5},{7,6},{8,7},{9,8},{10,9},{11,1... | collective-permute-start | bytes 4718600 | tf_op jit(solution)/shard_map/ppermute | solution.py:22
  46.1 14.6 %copy-start.16 = (f32[8,4]{0,1:T(4,128)S(1)}, f32[8,4]{0,1:T(4,128)}, u32[]{:S(2)}) copy-start(f32[8,4]{0,1:T(4,128)} %param.16) | copy-start | bytes 388
  47.8 281.2 %copy-start.8 = (bf16[1,4,1,128,256]{3,4,1,0,2:T(8,128)(2,1)S(1)}, bf16[1,4,1,128,256]{3,4,1,0,2:T(8,128)(2,1)}, u32[]{:S(2)}) copy-start(bf16[1,4,1,128,256]{3,4,1,0,2:T(8,128)(2,1)} %copy-done.7) | copy-start | bytes 786436
  47.8 281.2 %copy-start.10 = (bf16[1,4,1,128,256]{3,4,1,0,2:T(8,128)(2,1)S(1)}, bf16[1,4,1,128,256]{3,4,1,0,2:T(8,128)(2,1)}, u32[]{:S(2)}) copy-start(bf16[1,4,1,128,256]{3,4,1,0,2:T(8,128)(2,1)} %copy-done.9) | copy-start | bytes 786436
  47.9 3.7 collective-permute-start.8
  49.2 3.7 collective-permute-start.9
  52.9 62.5 %collective-permute-start.10 = (bf16[4,6,1,4,128]{4,1,0,3,2:T(8,128)(2,1)S(1)}, bf16[4,6,1,4,128]{4,1,0,3,2:T(8,128)(2,1)S(1)}, u32[]{:S(2)}, u32[]{:S(2)}) collective-permute-start(bf16[4,6,1,4,128]{4,1,0,3,2:T(8,128)(2,1)S(1)} %pad_maximum_fusion.14), channel_id=1, source_target_pairs={{0,1},{1,2},{2,3},{3,4},{4,5},{5,6},{6,7},{7,8},{8,9},{9,10},{10,1... | collective-permute-start | bytes 73736 | tf_op jit(solution)/shard_map/ppermute | solution.py:21
  53.0 62.4 %collective-permute-start.11 = (bf16[4,6,1,4,128]{4,1,0,3,2:T(8,128)(2,1)S(1)}, bf16[4,6,1,4,128]{4,1,0,3,2:T(8,128)(2,1)S(1)}, u32[]{:S(2)}, u32[]{:S(2)}) collective-permute-start(bf16[4,6,1,4,128]{4,1,0,3,2:T(8,128)(2,1)S(1)} %pad_maximum_fusion.14), channel_id=1, source_target_pairs={{1,0},{2,1},{3,2},{4,3},{5,4},{6,5},{7,6},{8,7},{9,8},{10,9},{11,1... | collective-permute-start | bytes 73736 | tf_op jit(solution)/shard_map/ppermute | solution.py:22
  628.7 3.2 copy-start.4
  628.7 3.2 copy-start.6
  (7 other events, 19.0 us)
Sparse Core Ops, SparseCore 0:
  48.0 278.0 all-reduce.1
where the time goes:
time: 645 us; the launch traced here: 642 us
  waiting for transfers between devices  270 us (42%)
  other arithmetic  135 us (21%)
  matrix products  126 us (20%)
  local copies, waits for them, and re-layouts  68 us (11%)
  starting transfers between devices  28.4 us (4%)
  between operations  13.7 us (2%)
    psum x1, waiting for transfers between devices, body(): wave_sums = lax.psum(partial_value, ('gx', 'gy', 'gz'))  211 us
    dot_general x27, matrix products, add_offset(): jnp.einsum('nhpq,nqhc->nphc', weights, near_feat, preferred_element_type=...  117 us
    exp x27, other arithmetic, pair_weights(): jnp.exp(-sharpness * jnp.square(distance - level_id / (level_count - 1)))  60.2 us
    ppermute x6, waiting for transfers between devices, padded(): before = lax.ppermute(last, axis, up)  56.9 us
    sub x27, other arithmetic, pair_weights(): near_geom[:, axis_id, None, :] + shift_vec[axis_id]  50.6 us
    dynamic_slice x27, local copies, waits for them, and re-layouts, add_offset(): lax.dynamic_slice(wide_feat, (step_x + 1, step_y + 1, step_z + 1, anchor,...  29.1 us
    ppermute x6, starting transfers between devices, padded(): after = lax.ppermute(first, axis, down)  23.5 us
    slice x27, local copies, waits for them, and re-layouts, pair_weights(): shift_vec[axis_id]  17.5 us
  transfers between devices with their start and end apart: 13, of which 6 were waited for; matrix products, arithmetic and copies ran while one was open for 3% of the time, Pallas kernels for 0%

commit v1 on v0

v1 whole, which is shorter than its diff:
```python
import math

import jax
import jax.numpy as jnp
from jax import lax
from jax.experimental import pallas as pl
from jax.experimental.pallas import tpu as pltpu
from jax.sharding import PartitionSpec as P

sharpness = 16.0
smearing = 0.04
screening = 4.0
strength = 24.0
BF = jnp.bfloat16
F32 = jnp.float32
LOG2E = 1.4426950408889634
REACH_SQ = sharpness * LOG2E
SCALE = math.sqrt(REACH_SQ)
FAR_AWAY = 1000.0
LEVELS = 8
STEP = 1.0 / (LEVELS - 1)
POWER = 2.0 * sharpness * STEP * LOG2E / SCALE
VMEM = 56 * 1024 * 1024


def bumps(home, row, shift, eye):
    dist_sq = None
    for a in range(3):
        gap = (row[a] + shift[a]) - home[a]
        dist_sq = gap * gap if dist_sq is None else dist_sq + gap * gap
    dist_sq = jnp.minimum(dist_sq, REACH_SQ)
    if eye is not None:
        dist_sq = jnp.where(eye, REACH_SQ, dist_sq)
    rise = REACH_SQ - dist_sq
    distance = dist_sq * lax.rsqrt(jnp.maximum(dist_sq, 1e-30))
    ratio = jnp.exp2(POWER * distance)
    value = rise * rise * jnp.exp2(-dist_sq)
    values = [value]
    for _ in range(LEVELS - 1):
        value = value * ratio
        values.append(value)
    return values


def pair_kernel(own, first, *refs):
    if first:
        feat_ref, row_ref, home_ref, weight_ref, acc_ref, y_ref, fw_ref = refs
    else:
        feat_ref, row_ref, home_ref, weight_ref, old_ref, acc_ref, y_ref, fw_ref = refs
    source = pl.program_id(0)
    sx = source // 4
    sy = source % 4

    @pl.when(source == 0)
    def _():
        if first:
            acc_ref[...] = jnp.zeros_like(acc_ref)
        else:
            acc_ref[...] = old_ref[...]

    feat = feat_ref[0].astype(F32)
    for b in range(LEVELS):
        fw_ref[b * 128 : (b + 1) * 128, :] = (feat * weight_ref[b : b + 1, :]).astype(BF)
    row = [row_ref[0, a : a + 1, :] for a in range(3)]
    rows = 32
    for j in range(9):
        jx, jy = j // 3, j % 3
        cell = (sx + jx) * 6 + sy + jy
        shift = ((1 - jx) * SCALE, (1 - jy) * SCALE, 0.0)
        for r in range(128 // rows):
            cols = home_ref[cell, r * rows : (r + 1) * rows, :]
            home = [cols[:, a : a + 1] for a in range(3)]
            eye = None
            if own and j == 4:
                eye = lax.broadcasted_iota(jnp.int32, (rows, 128), 0) + r * rows == (
                    lax.broadcasted_iota(jnp.int32, (rows, 128), 1)
                )
            values = bumps(home, row, shift, eye)
            for b in range(LEVELS):
                y_ref[j * 128 + r * rows : j * 128 + (r + 1) * rows, b * 128 : (b + 1) * 128] = (
                    values[b].astype(BF)
                )
    out = jnp.dot(y_ref[...], fw_ref[...], preferred_element_type=F32)
    for j in range(9):
        cell = (sx + j // 3) * 6 + sy + j % 3
        acc_ref[cell] += out[j * 128 : (j + 1) * 128]


def pair_messages(feat, row, home, weight, old, own, name):
    first = old is None
    whole = pl.BlockSpec((24, 128, 256), lambda s: (0, 0, 0))
    in_specs = [
        pl.BlockSpec((1, 128, 256), lambda s: (s, 0, 0)),
        pl.BlockSpec((1, 8, 128), lambda s: (s, 0, 0)),
        pl.BlockSpec((24, 128, 8), lambda s: (0, 0, 0)),
        pl.BlockSpec((8, 256), lambda s: (0, 0)),
    ]
    args = [feat, row, home, weight]
    aliases = {}
    if not first:
        in_specs.append(whole)
        args.append(old)
        aliases = {4: 0}

    def kernel(*refs):
        pair_kernel(own, first, *refs)

    return pl.pallas_call(
        kernel,
        grid=(8,),
        in_specs=in_specs,
        out_specs=whole,
        out_shape=jax.ShapeDtypeStruct((24, 128, 256), F32),
        scratch_shapes=[pltpu.VMEM((1152, 1024), BF), pltpu.VMEM((1024, 256), BF)],
        input_output_aliases=aliases,
        compiler_params=pltpu.CompilerParams(
            dimension_semantics=("arbitrary",), vmem_limit_bytes=VMEM
        ),
        name=name,
    )(*args)


SIN = [
    math.pi * (-1) ** i * math.pi ** (2 * i) / math.factorial(2 * i + 1) for i in range(7)
]
COS = [(-1) ** i * math.pi ** (2 * i) / math.factorial(2 * i) for i in range(7)]


def cos_sin(turns):
    part = turns - jnp.floor(turns + 0.5)
    sq = part * part
    sin_half = jnp.full_like(sq, SIN[-1])
    cos_half = jnp.full_like(sq, COS[-1])
    for i in range(len(SIN) - 2, -1, -1):
        sin_half = sin_half * sq + SIN[i]
        cos_half = cos_half * sq + COS[i]
    sin_half = sin_half * part
    twice = sin_half + sin_half
    return 1.0 - twice * sin_half, twice * cos_half


def structure_kernel(feat_ref, row_ref, wave_ref, out_ref, bt_ref):
    for c in range(16):
        waves = wave_ref[c * 32 : (c + 1) * 32, :]
        wave = [jnp.broadcast_to(waves[:, a : a + 1], (32, 128)) for a in range(3)]
        for n in range(8):
            turns = None
            for a in range(3):
                term = wave[a] * row_ref[n, 4 + a : 5 + a, :]
                turns = term if turns is None else turns + term
            cos, sin = cos_sin(turns)
            mask = row_ref[n, 3:4, :]
            bt_ref[c * 64 : c * 64 + 32, n * 128 : (n + 1) * 128] = (cos * mask).astype(BF)
            bt_ref[c * 64 + 32 : c * 64 + 64, n * 128 : (n + 1) * 128] = (sin * mask).astype(BF)
    out_ref[...] = jnp.dot(bt_ref[...], feat_ref[...], preferred_element_type=F32).astype(BF)


def structure(feat, row, wave_cols):
    return pl.pallas_call(
        structure_kernel,
        out_shape=jax.ShapeDtypeStruct((1024, 256), BF),
        scratch_shapes=[pltpu.VMEM((1024, 1024), BF)],
        compiler_params=pltpu.CompilerParams(vmem_limit_bytes=VMEM),
        name="structure",
    )(feat, row, wave_cols)


def basis_kernel(home_ref, wave_ref, out_ref):
    for r in range(4):
        cols = home_ref[0, r * 32 : (r + 1) * 32, :]
        place = [jnp.broadcast_to(cols[:, 4 + a : 5 + a], (32, 128)) for a in range(3)]
        for c in range(4):
            turns = None
            for a in range(3):
                term = place[a] * wave_ref[a : a + 1, c * 128 : (c + 1) * 128]
                turns = term if turns is None else turns + term
            cos, sin = cos_sin(turns)
            out_ref[r * 32 : (r + 1) * 32, c * 256 : c * 256 + 128] = cos.astype(BF)
            out_ref[r * 32 : (r + 1) * 32, c * 256 + 128 : c * 256 + 256] = sin.astype(BF)


def basis(home, wave_rows):
    return pl.pallas_call(
        basis_kernel,
        grid=(8,),
        in_specs=[
            pl.BlockSpec((1, 128, 8), lambda n: ((n // 4 + 1) * 6 + n % 4 + 1, 0, 0)),
            pl.BlockSpec((8, 512), lambda n: (0, 0)),
        ],
        out_specs=pl.BlockSpec((128, 1024), lambda n: (n, 0)),
        out_shape=jax.ShapeDtypeStruct((1024, 1024), BF),
        compiler_params=pltpu.CompilerParams(vmem_limit_bytes=VMEM),
        name="wave_basis",
    )(home, wave_rows)


def update_kernel(
    basis_ref, f0, f1, f2, f3, acc_ref, y0, y3, x0, x1, feat_ref, home_ref, mw, ew, ow, out_ref
):
    half = pl.program_id(0)
    values = None
    for i, f in enumerate((f0, f1, f2, f3)):
        part = jnp.dot(
            basis_ref[:, i * 256 : (i + 1) * 256], f[...], preferred_element_type=F32
        )
        values = part if values is None else values + part
    ewald = values.astype(BF)
    cells = []
    for y in range(4):
        total = acc_ref[0, y + 1]
        if y == 0:
            total = total + y0[0].astype(F32)
        if y == 3:
            total = total + y3[0].astype(F32)
        total = total + jnp.where(half == 0, x0[y].astype(F32), x1[y].astype(F32))
        cells.append(total.astype(BF))
    messages = jnp.concatenate(cells, axis=0)
    joined = jnp.dot(messages, mw[...], preferred_element_type=F32) + jnp.dot(
        ewald, ew[...], preferred_element_type=F32
    )
    hidden = (joined / (1.0 + jnp.exp(-joined))).astype(BF)
    update = jnp.dot(hidden, ow[...], preferred_element_type=F32)
    for y in range(4):
        rows = slice(y * 128, (y + 1) * 128)
        mask = home_ref[0, y + 1, :, 3:4]
        out_ref[y] = ((feat_ref[y].astype(F32) + update[rows]) * mask).astype(BF)


def update(base, filt, acc, y_low, y_high, x_low, x_high, feat, home, mw, ew, ow):
    full = lambda shape: pl.BlockSpec(shape, lambda i: (0,) * len(shape))
    return pl.pallas_call(
        update_kernel,
        grid=(2,),
        in_specs=[
            pl.BlockSpec((512, 1024), lambda i: (i, 0)),
            full((256, 256)),
            full((256, 256)),
            full((256, 256)),
            full((256, 256)),
            pl.BlockSpec((1, 6, 128, 256), lambda i: (i + 1, 0, 0, 0)),
            pl.BlockSpec((1, 128, 256), lambda i: (i + 1, 0, 0)),
            pl.BlockSpec((1, 128, 256), lambda i: (i + 1, 0, 0)),
            full((4, 128, 256)),
            full((4, 128, 256)),
            pl.BlockSpec((4, 128, 256), lambda i: (i, 0, 0)),
            pl.BlockSpec((1, 6, 128, 8), lambda i: (i + 1, 0, 0, 0)),
            full((256, 256)),
            full((256, 256)),
            full((256, 256)),
        ],
        out_specs=pl.BlockSpec((4, 128, 256), lambda i: (i, 0, 0)),
        out_shape=jax.ShapeDtypeStruct((8, 128, 256), BF),
        compiler_params=pltpu.CompilerParams(vmem_limit_bytes=VMEM),
        name="update",
    )(
        base,
        *filt,
        acc.reshape(4, 6, 128, 256),
        y_low,
        y_high,
        x_low,
        x_high,
        feat,
        home.reshape(4, 6, 128, 8),
        mw,
        ew,
        ow,
    )


def shifted(count, step):
    return [(i, (i + step) % count) for i in range(count)]


def high_digit(step):
    return [(i, (i // 4 + step) % 4 * 4 + i % 4) for i in range(16)]


def low_digit(step):
    return [(i, i ^ step) for i in range(16)]


def far_pairs():
    return [(i, (i + 1) % 16 if i % 2 else (i - 1) % 16) for i in range(16)]


def body(
    features,
    fractions,
    occupied,
    wave_index,
    radial_weight,
    ewald_mix,
    msg_weight,
    ewald_weight,
    out_weight,
):
    gx, gy, gz = (lax.axis_index(name) for name in ("gx", "gy", "gz"))
    feat = features.reshape(8, 128, 256)
    frac = fractions.reshape(2, 4, 3, 128)
    mask = occupied.reshape(8, 1, 128).astype(BF)
    geometry = jnp.concatenate([frac.reshape(8, 3, 128), mask], axis=1)

    near_geom = lax.ppermute(geometry, "gz", low_digit(1))
    near_feat = lax.ppermute(feat, "gz", low_digit(1))
    far_geom = lax.ppermute(geometry, "gz", far_pairs())
    far_feat = lax.ppermute(feat, "gz", far_pairs())

    left = lax.ppermute(frac[1:], "gx", shifted(4, 1))
    right = lax.ppermute(frac[:1], "gx", shifted(4, -1))
    wide = jnp.concatenate([left, frac, right], axis=0)
    below = lax.ppermute(wide[:, 3:], "gy", shifted(4, 1))
    above = lax.ppermute(wide[:, :1], "gy", shifted(4, -1))
    wide = jnp.concatenate([below, wide, above], axis=1)

    occ = mask.astype(F32)
    starts = jnp.stack(
        [
            jnp.broadcast_to((gx * 2 + jnp.arange(2))[:, None], (2, 4)),
            jnp.broadcast_to((gy * 4 + jnp.arange(4))[None, :], (2, 4)),
            jnp.broadcast_to(gz, (2, 4)),
        ],
        axis=-1,
    ).astype(F32)
    lengths = jnp.array([8.0, 16.0, 16.0], F32)
    place = (starts[..., None] + frac.astype(F32)) / lengths[:, None]

    def source_rows(geom, lift):
        pos = geom[:, :3].astype(F32) * SCALE
        hide = (1.0 - geom[:, 3:].astype(F32)) * FAR_AWAY
        return jnp.concatenate(
            [pos[:, :1] + hide, pos[:, 1:2], pos[:, 2:] + lift * SCALE, geom[:, 3:].astype(F32)],
            axis=1,
        )

    core_sign = 1.0 - 2.0 * (gz % 2).astype(F32)
    own_rows = jnp.concatenate(
        [source_rows(geometry, 0.0), place.reshape(8, 3, 128), jnp.zeros((8, 1, 128), F32)], axis=1
    )
    pad_rows = lambda rows: jnp.concatenate([rows, jnp.zeros((8, 4, 128), F32)], axis=1)
    near_rows = pad_rows(source_rows(near_geom, core_sign))
    far_rows = pad_rows(source_rows(far_geom, -core_sign))

    own_extra = jnp.concatenate(
        [occ.reshape(2, 4, 1, 128), place, jnp.zeros((2, 4, 1, 128), F32)], axis=2
    )
    own_extra = jnp.pad(own_extra, ((1, 1), (1, 1), (0, 0), (0, 0)))
    home = jnp.concatenate([wide.astype(F32) * SCALE, own_extra], axis=2)
    home = home.reshape(24, 8, 128).transpose(0, 2, 1)

    level = jnp.arange(LEVELS, dtype=F32)[:, None] * STEP
    weight = radial_weight * jnp.exp(-sharpness * level * level)
    weight = weight * (1.0 / (REACH_SQ * REACH_SQ * math.sqrt(512.0)))
    weight = jnp.repeat(weight, 64, axis=1)

    blocks = wave_index.astype(F32).reshape(3, 4, 4, 32)

    def turned(values, axis, start):
        twice = jnp.concatenate([values, values], axis=axis)
        return lax.dynamic_slice_in_dim(twice, start, 4, axis=axis)

    sent = turned(turned(blocks, 1, gy), 2, gx)
    wave_cols = jnp.pad(sent.reshape(3, 512).T, ((0, 0), (0, 5)))
    come = turned(turned(blocks[:, ::-1, ::-1], 1, 3 - gy), 2, 3 - gx)
    wave_rows = jnp.pad(come.reshape(3, 512), ((0, 5), (0, 0)))

    terms = structure(feat.reshape(1024, 256), own_rows, wave_cols).reshape(4, 256, 256)
    got = [lax.ppermute(terms[s], "gy", shifted(4, s)) for s in (1, 2, 3)]
    acc = pair_messages(feat, own_rows, home, weight, None, True, "pair_own")
    sums = terms[0].astype(F32) + got[0].astype(F32) + got[1].astype(F32) + got[2].astype(F32)
    sums = sums.astype(BF).reshape(4, 64, 256)
    got = [lax.ppermute(sums[r], "gx", shifted(4, r)) for r in (1, 2, 3)]
    acc = pair_messages(near_feat, near_rows, home, weight, acc, False, "pair_near")
    sums = sums[0].astype(F32) + got[0].astype(F32) + got[1].astype(F32) + got[2].astype(F32)
    sent_sums = sums.astype(BF)
    got = [lax.ppermute(sent_sums, "gz", high_digit(s)) for s in (1, 2, 3)]
    sums = sums + got[0].astype(F32) + got[1].astype(F32) + got[2].astype(F32)
    sent_sums = sums.astype(BF)
    got = [lax.ppermute(sent_sums, "gz", low_digit(s)) for s in (1, 2, 3)]
    sums = sums + got[0].astype(F32) + got[1].astype(F32) + got[2].astype(F32)

    wave_vec = 2.0 * math.pi * sent[:, 0, 0] / lengths[:, None]
    wave_sq = jnp.sum(wave_vec * wave_vec, axis=0)
    damping = (
        strength
        * jnp.exp(-0.5 * smearing * wave_sq)
        / (wave_sq + screening)
        * (1.0 / math.sqrt(262144 * 512))
    )
    mixed = jnp.dot(sums, ewald_mix, precision=lax.Precision.HIGHEST)
    filtered = (mixed.reshape(2, 32, 256) * damping[None, :, None]).astype(BF)
    filtered = [filtered] + [lax.ppermute(filtered, "gx", shifted(4, r)) for r in (1, 2, 3)]
    filtered = jnp.stack(filtered, axis=1).reshape(256, 256)
    filtered = [filtered] + [lax.ppermute(filtered, "gy", shifted(4, s)) for s in (1, 2, 3)]

    base = basis(home, wave_rows)
    acc = pair_messages(far_feat, far_rows, home, weight, acc, False, "pair_far")
    wide_acc = acc.reshape(4, 6, 128, 256)
    y_high = lax.ppermute(wide_acc[:, 0].astype(BF), "gy", shifted(4, -1))
    y_low = lax.ppermute(wide_acc[:, 5].astype(BF), "gy", shifted(4, 1))

    def edge(x):
        cells = [wide_acc[x, 1] + y_low[x].astype(F32), wide_acc[x, 2]]
        cells += [wide_acc[x, 3], wide_acc[x, 4] + y_high[x].astype(F32)]
        return jnp.stack(cells).astype(BF)

    x_high = lax.ppermute(edge(0), "gx", shifted(4, -1))
    x_low = lax.ppermute(edge(3), "gx", shifted(4, 1))
    out = update(
        base,
        filtered,
        acc,
        y_low,
        y_high,
        x_low,
        x_high,
        feat,
        home,
        msg_weight,
        ewald_weight,
        out_weight,
    )
    return out.reshape(features.shape)


def solution(mesh):
    in_specs = (
        P("gx", "gy", "gz", None, None),
        P("gx", "gy", "gz", None, None),
        P("gx", "gy", "gz", None),
        P(),
        P(),
        P(),
        P(),
        P(),
        P(),
    )
    out_specs = P("gx", "gy", "gz", None, None)
    return jax.shard_map(body, mesh=mesh, in_specs=in_specs, out_specs=out_specs, check_vma=False)
```

time: 645 us -> 160 us (0.25)
  waiting for transfers between devices: 270 us -> 24 us
  other arithmetic: 135 us -> 8.91 us
  matrix products: 126 us -> 0.25 us
  Pallas kernels: 0 us -> 65.1 us
  local copies, waits for them, and re-layouts: 68 us -> 11.8 us
  starting transfers between devices: 28.4 us -> 48.1 us
  between operations: 13.7 us -> 0.39 us
    psum x1 -> x0, waiting for transfers between devices: 211 us -> none  [body(): wave_sums = lax.psum(partial_value, ('gx', 'gy', 'gz'))]
    dot_general x32 -> x1, matrix products: 126 us -> 0.25 us  [body(): mixed = jnp.dot(sums, ewald_mix, precision=lax.Precision.HIGHEST)]
    pallas_call x0 -> x6, Pallas kernels: none -> 65.1 us  [the longest x3 47.8 us: pair_messages(): pl.pallas_call(kernel, grid=(8,), in_specs=in_specs, out_specs=whole, out...]
    exp x27 -> x1, other arithmetic: 60.2 us -> 0.01 us  [body(): weight = radial_weight * jnp.exp(-sharpness * level * level)]
    sub x54 -> x0, other arithmetic: 51 us -> none  [the longest x27 50.6 us: pair_weights(): near_geom[:, axis_id, None, :] + shift_vec[axis_id]]
    ppermute x12 -> x30, waiting for transfers between devices: 59.3 us -> 24 us  [the longest x1 5.68 us: body(): y_low = lax.ppermute(wide_acc[:, 5].astype(BF), 'gy', shifted(4, 1))]
    dynamic_slice x54 -> x1, local copies, waits for them, and re-layouts: 29.4 us -> 0.18 us  [turned(): return lax.dynamic_slice_in_dim(twice, start, 4, axis=axis)]
    ppermute x12 -> x30, starting transfers between devices: 28.4 us -> 48.1 us  [the longest x1 9.74 us: body(): far_geom = lax.ppermute(geometry, 'gz', far_pairs())]
  transfers between devices with their start and end apart: 13 -> 30, of which waited for: 6 -> 13; matrix products, arithmetic and copies ran while one was open for 3% -> 11% of each run, Pallas kernels for 0% -> 38%
where the time goes in v1:
time: 160 us; the launch traced here: 159 us
  Pallas kernels  65.1 us (41%)
  starting transfers between devices  48.1 us (30%)
  waiting for transfers between devices  24 us (15%)
  local copies, waits for them, and re-layouts  11.8 us (7%)
  other arithmetic  8.91 us (6%)
    pallas_call x3, Pallas kernels, pair_messages(): pl.pallas_call(kernel, grid=(8,), in_specs=in_specs, out_specs=whole, out...  47.8 us
    ppermute x1, starting transfers between devices, body(): far_geom = lax.ppermute(geometry, 'gz', far_pairs())  9.74 us
    pallas_call x1, Pallas kernels, basis(): pl.pallas_call(basis_kernel, grid=(8,), in_specs=[pl.BlockSpec((1, 128, 8...  6.71 us
    ppermute x3, starting transfers between devices, body(): got = [lax.ppermute(sent_sums, 'gz', low_digit(s)) for s in (1, 2, 3)]  5.87 us
    ppermute x1, waiting for transfers between devices, body(): y_low = lax.ppermute(wide_acc[:, 5].astype(BF), 'gy', shifted(4, 1))  5.68 us
    ppermute x3, starting transfers between devices, body(): lax.ppermute(filtered, 'gy', shifted(4, s))  5.47 us
    pallas_call x1, Pallas kernels, structure(): pl.pallas_call(structure_kernel, out_shape=jax.ShapeDtypeStruct((1024, 25...  5.36 us
    ppermute x3, waiting for transfers between devices, body(): got = [lax.ppermute(sent_sums, 'gz', low_digit(s)) for s in (1, 2, 3)]  5.3 us
  transfers between devices with their start and end apart: 30, of which 13 were waited for; matrix products, arithmetic and copies ran while one was open for 11% of the time, Pallas kernels for 38%

profile of v1, /device:TPU:2, one launch (start us, length us, event | category | flops | bytes accessed | tf_op | source)
XLA Modules:
  0.0 158.5 jit_solution(6623640390913961328)
XLA Ops:
  1.6 9.7 %collective-permute-start.23 = (bf16[8,4,128]{2,1,0:T(4,128)(2,1)S(1)}, bf16[8,4,128]{2,1,0:T(4,128)(2,1)S(1)}, u32[]{:S(2)}, u32[]{:S(2)}) collective-permute-start(bf16[8,4,128]{2,1,0:T(4,128)(2,1)S(1)} %pad_maximum_fusion.4), channel_id=1, source_target_pairs={{0,15},{1,2},{2,1},{3,4},{4,3},{5,6},{6,5},{7,8},{8,7},{9,10},{10,... | collective-permute-start | bytes 24584 | tf_op jit(solution)/shard_map/ppermute | solution.py:306
  13.1 2.8 %collective-permute-start.1 = (bf16[1,4,3,128]{3,1,2,0:T(4,128)(2,1)S(1)}, bf16[1,4,3,128]{3,1,2,0:T(4,128)(2,1)S(1)}, u32[]{:S(2)}, u32[]{:S(2)}) collective-permute-start(bf16[1,4,3,128]{3,1,2,0:T(4,128)(2,1)S(1)} %get-tuple-element.36), channel_id=1, source_target_pairs={{0,192},{64,0},{128,64},{192,128},{1,193},{65,1},{129,65},{193,129... | collective-permute-start | bytes 9224 | tf_op jit(solution)/shard_map/ppermute | solution.py:310
  21.2 5.4 %structure.1 = bf16[1024,256]{1,0:T(8,128)(2,1)} custom-call(bf16[1024,256]{1,0:T(8,128)(2,1)} %bitcast.97, f32[8,8,128]{2,1,0:T(8,128)} %concatenate.47.row_ref.refs_1_, f32[512,8]{1,0:T(8,128)} %pad.14.wave_ref), custom_call_target="tpu_custom_call" | custom-call | tf_op jit(solution)/shard_map/structure/pallas_call | solution.py:159
  36.1 15.3 %pair_own.1.refs_4_ = f32[24,128,256]{2,1,0:T(8,128)} custom-call(bf16[8,128,256]{2,1,0:T(8,128)(2,1)} %bitcast.98, f32[8,8,128]{2,1,0:T(8,128)} %concatenate.47.row_ref.refs_1_, f32[24,128,8]{2,1,0:T(8,128)} %bitcast.91, f32[8,256]{1,0:T(8,128)} %reshape.173.refs_3_), custom_call_target="tpu_custom_call" | custom-call | tf_op jit(solution)/shard_map/pair_own/pallas_call | solution.py:108
  52.8 2.4 %collective-permute-start.6 = (bf16[256,256]{1,0:T(8,128)(2,1)S(1)}, bf16[256,256]{1,0:T(8,128)(2,1)S(1)}, u32[]{:S(2)}, u32[]{:S(2)}) collective-permute-start(bf16[256,256]{1,0:T(8,128)(2,1)S(1)} %get-tuple-element.20), channel_id=1, source_target_pairs={{0,48},{16,0},{32,16},{48,32},{1,49},{17,1},{33,17},{49,33},{2,50}... | collective-permute-start | bytes 393224 | tf_op jit(solution)/shard_map/ppermute | solution.py:368
  55.2 3.3 %collective-permute-done.5 = bf16[256,256]{1,0:T(8,128)(2,1)S(1)} collective-permute-done((bf16[256,256]{1,0:T(8,128)(2,1)S(1)}, bf16[256,256]{1,0:T(8,128)(2,1)S(1)}, u32[]{:S(2)}, u32[]{:S(2)}) %collective-permute-start.5) | collective-permute-done | bytes 131104 | tf_op jit(solution)/shard_map/ppermute | solution.py:368
  61.6 3.1 %collective-permute-start.9 = (bf16[64,256]{1,0:T(8,128)(2,1)S(1)}, bf16[64,256]{1,0:T(8,128)(2,1)S(1)}, u32[]{:S(2)}, u32[]{:S(2)}) collective-permute-start(bf16[64,256]{1,0:T(8,128)(2,1)S(1)} %get-tuple-element.23), channel_id=1, source_target_pairs={{0,192},{64,0},{128,64},{192,128},{1,193},{65,1},{129,65},{193,129... | collective-permute-start | bytes 98312 | tf_op jit(solution)/shard_map/ppermute | solution.py:372
  64.8 2.0 %collective-permute-done.7 = bf16[64,256]{1,0:T(8,128)(2,1)S(1)} collective-permute-done((bf16[64,256]{1,0:T(8,128)(2,1)S(1)}, bf16[64,256]{1,0:T(8,128)(2,1)S(1)}, u32[]{:S(2)}, u32[]{:S(2)}) %collective-permute-start.7) | collective-permute-done | bytes 32800 | tf_op jit(solution)/shard_map/ppermute | solution.py:372
  67.3 2.2 %collective-permute-start.11 = (bf16[64,256]{1,0:T(8,128)(2,1)S(1)}, bf16[64,256]{1,0:T(8,128)(2,1)S(1)}, u32[]{:S(2)}, u32[]{:S(2)}) collective-permute-start(bf16[64,256]{1,0:T(8,128)(2,1)S(1)} %fusion.19), channel_id=1, source_target_pairs={{0,8},{1,9},{2,10},{3,11},{4,12},{5,13},{6,14},{7,15},{8,0},{9,1},... | collective-permute-start | bytes 98312 | tf_op jit(solution)/shard_map/ppermute | solution.py:376
  70.7 1.7 %collective-permute-done.10 = bf16[64,256]{1,0:T(8,128)(2,1)S(1)} collective-permute-done((bf16[64,256]{1,0:T(8,128)(2,1)S(1)}, bf16[64,256]{1,0:T(8,128)(2,1)S(1)}, u32[]{:S(2)}, u32[]{:S(2)}) %collective-permute-start.10) | collective-permute-done | bytes 32800 | tf_op jit(solution)/shard_map/ppermute | solution.py:376
  73.8 5.1 %collective-permute-start.14 = (bf16[64,256]{1,0:T(8,128)(2,1)S(1)}, bf16[64,256]{1,0:T(8,128)(2,1)S(1)}, u32[]{:S(2)}, u32[]{:S(2)}) collective-permute-start(bf16[64,256]{1,0:T(8,128)(2,1)S(1)} %get-tuple-element.5), channel_id=1, source_target_pairs={{0,2},{1,3},{2,0},{3,1},{4,6},{5,7},{6,4},{7,5},{8,10},{9,11},{10,... | collective-permute-start | bytes 98312 | tf_op jit(solution)/shard_map/ppermute | solution.py:379
  81.7 4.5 %collective-permute-done.15 = bf16[64,256]{1,0:T(8,128)(2,1)S(1)} collective-permute-done((bf16[64,256]{1,0:T(8,128)(2,1)S(1)}, bf16[64,256]{1,0:T(8,128)(2,1)S(1)}, u32[]{:S(2)}, u32[]{:S(2)}) %collective-permute-start.15) | collective-permute-done | bytes 32800 | tf_op jit(solution)/shard_map/ppermute | solution.py:379
  86.5 1.9 %collective-permute-start.16 = (bf16[2,32,256]{2,1,0:T(8,128)(2,1)S(1)}, bf16[2,32,256]{2,1,0:T(8,128)(2,1)S(1)}, u32[]{:S(2)}, u32[]{:S(2)}) collective-permute-start(bf16[2,32,256]{2,1,0:T(8,128)(2,1)S(1)} %multiply_convert_fusion), channel_id=1, source_target_pairs={{0,64},{64,128},{128,192},{192,0},{1,65},{65,129},{129,193},{193,1... | collective-permute-start | bytes 98312 | tf_op jit(solution)/shard_map/ppermute | solution.py:392
  88.4 1.8 %collective-permute-start.17 = (bf16[2,32,256]{2,1,0:T(8,128)(2,1)S(1)}, bf16[2,32,256]{2,1,0:T(8,128)(2,1)S(1)}, u32[]{:S(2)}, u32[]{:S(2)}) collective-permute-start(bf16[2,32,256]{2,1,0:T(8,128)(2,1)S(1)} %multiply_convert_fusion), channel_id=1, source_target_pairs={{0,128},{64,192},{128,0},{192,64},{1,129},{65,193},{129,1},{193,65... | collective-permute-start | bytes 98312 | tf_op jit(solution)/shard_map/ppermute | solution.py:392
  91.6 16.3 %pair_near.1.refs_4_ = f32[24,128,256]{2,1,0:T(8,128)} custom-call(bf16[8,128,256]{2,1,0:T(8,128)(2,1)} %copy-done.5, f32[8,8,128]{2,1,0:T(8,128)} %concatenate.52.refs_1_, f32[24,128,8]{2,1,0:T(8,128)} %bitcast.92, f32[8,256]{1,0:T(8,128)} %reshape.173.refs_3_, f32[24,128,256]{2,1,0:T(8,128)} %pair_own.1.refs_4_), custom_call_target="tpu_custom_call", output_to_operand_aliasing={{}: (4, {})} | custom-call | tf_op jit(solution)/shard_map/pair_near/pallas_call | solution.py:108
  108.7 16.3 %pair_far.1 = f32[24,128,256]{2,1,0:T(8,128)} custom-call(bf16[8,128,256]{2,1,0:T(8,128)(2,1)} %copy-done.6, f32[8,8,128]{2,1,0:T(8,128)} %concatenate.51.refs_1_, f32[24,128,8]{2,1,0:T(8,128)} %bitcast.93, f32[8,256]{1,0:T(8,128)} %reshape.173.refs_3_, f32[24,128,256]{2,1,0:T(8,128)} %pair_near.1.refs_4_), custom_call_target="tpu_custom_call", output_to_operand_aliasing={{}: (4, {})} | custom-call | tf_op jit(solution)/shard_map/pair_far/pallas_call | solution.py:108
  125.0 2.1 %convert.28 = bf16[4,6,128,256]{3,2,1,0:T(8,128)(2,1)S(1)} convert(f32[4,6,128,256]{3,2,1,0:T(8,128)} %bitcast.88) | non-fusion elementwise | flops 786432 | bytes 4718592 | tf_op jit(solution)/shard_map/convert.17
  127.4 1.8 %collective-permute-start.27 = (bf16[4,128,256]{2,1,0:T(8,128)(2,1)S(1)}, bf16[4,128,256]{2,1,0:T(8,128)(2,1)S(1)}, u32[]{:S(2)}, u32[]{:S(2)}) collective-permute-start(bf16[4,128,256]{2,1,0:T(8,128)(2,1)S(1)} %get-tuple-element.17), channel_id=1, source_target_pairs={{0,48},{16,0},{32,16},{48,32},{1,49},{17,1},{33,17},{49,33},{2,50}... | collective-permute-start | bytes 786440 | tf_op jit(solution)/shard_map/ppermute | solution.py:399
  129.3 5.7 %collective-permute-done.26.y0 = bf16[4,128,256]{2,1,0:T(8,128)(2,1)S(1)} collective-permute-done((bf16[4,128,256]{2,1,0:T(8,128)(2,1)S(1)}, bf16[4,128,256]{2,1,0:T(8,128)(2,1)S(1)}, u32[]{:S(2)}, u32[]{:S(2)}) %collective-permute-start.26) | collective-permute-done | bytes 262176 | tf_op jit(solution)/shard_map/ppermute | solution.py:400
  137.1 1.7 %collective-permute-start.29 = (bf16[4,128,256]{2,1,0:T(8,128)(2,1)S(1)}, bf16[4,128,256]{2,1,0:T(8,128)(2,1)S(1)}, u32[]{:S(2)}, u32[]{:S(2)}) collective-permute-start(bf16[4,128,256]{2,1,0:T(8,128)(2,1)S(1)} %pad_maximum_fusion.1), channel_id=1, source_target_pairs={{0,192},{64,0},{128,64},{192,128},{1,193},{65,1},{129,65},{193,129... | collective-permute-start | bytes 786440 | tf_op jit(solution)/shard_map/ppermute | solution.py:407
  139.3 1.8 %collective-permute-start.19 = (bf16[256,256]{1,0:T(8,128)(2,1)S(1)}, bf16[256,256]{1,0:T(8,128)(2,1)S(1)}, u32[]{:S(2)}, u32[]{:S(2)}) collective-permute-start(bf16[256,256]{1,0:T(8,128)(2,1)S(1)} %bitcast.104), channel_id=1, source_target_pairs={{0,16},{16,32},{32,48},{48,0},{1,17},{17,33},{33,49},{49,1},{2,18}... | collective-permute-start | bytes 393224 | tf_op jit(solution)/shard_map/ppermute | solution.py:394
  142.5 2.3 %collective-permute-start.21 = (bf16[256,256]{1,0:T(8,128)(2,1)S(1)}, bf16[256,256]{1,0:T(8,128)(2,1)S(1)}, u32[]{:S(2)}, u32[]{:S(2)}) collective-permute-start(bf16[256,256]{1,0:T(8,128)(2,1)S(1)} %bitcast.106), channel_id=1, source_target_pairs={{0,48},{16,0},{32,16},{48,32},{1,49},{17,1},{33,17},{49,33},{2,50}... | collective-permute-start | bytes 393224 | tf_op jit(solution)/shard_map/ppermute | solution.py:394
  145.6 6.7 %wave_basis.1.basis_ref = bf16[1024,1024]{1,0:T(8,128)(2,1)} custom-call(f32[24,128,8]{2,1,0:T(8,128)} %bitcast.94, f32[8,512]{1,0:T(8,128)} %pad.13.wave_ref), custom_call_target="tpu_custom_call" | custom-call | tf_op jit(solution)/shard_map/wave_basis/pallas_call | solution.py:183
  153.3 5.2 %update.1 = bf16[8,128,256]{2,1,0:T(8,128)(2,1)} custom-call(bf16[1024,1024]{1,0:T(8,128)(2,1)} %wave_basis.1.basis_ref, bf16[256,256]{1,0:T(8,128)(2,1)} %bitcast.107, bf16[256,256]{1,0:T(8,128)(2,1)} %copy-done.10, bf16[256,256]{1,0:T(8,128)(2,1)} %copy-done.11, bf16[256,256]{1,0:T(8,128)(2,1)} %copy-done.12, f32[4,6,128,256]{3,2,1,0:T(8,128)} %bitcast.90, ...), custom_call_target="tpu_custom_call" | custom-call | tf_op jit(solution)/shard_map/update/pallas_call | solution.py:231
  (144 shorter events, 37.0 us)
Async XLA Ops:
  1.5 49.8 %collective-permute-start.25 = (bf16[8,4,128]{2,1,0:T(4,128)(2,1)S(1)}, bf16[8,4,128]{2,1,0:T(4,128)(2,1)S(1)}, u32[]{:S(2)}, u32[]{:S(2)}) collective-permute-start(bf16[8,4,128]{2,1,0:T(4,128)(2,1)S(1)} %pad_maximum_fusion.4), channel_id=1, source_target_pairs={{0,1},{1,0},{2,3},{3,2},{4,5},{5,4},{6,7},{7,6},{8,9},{9,8},{10,11... | collective-permute-start | bytes 24584 | tf_op jit(solution)/shard_map/ppermute | solution.py:304
  1.6 51.1 %collective-permute-start.23 = (bf16[8,4,128]{2,1,0:T(4,128)(2,1)S(1)}, bf16[8,4,128]{2,1,0:T(4,128)(2,1)S(1)}, u32[]{:S(2)}, u32[]{:S(2)}) collective-permute-start(bf16[8,4,128]{2,1,0:T(4,128)(2,1)S(1)} %pad_maximum_fusion.4), channel_id=1, source_target_pairs={{0,15},{1,2},{2,1},{3,4},{4,3},{5,6},{6,5},{7,8},{8,7},{9,10},{10,... | collective-permute-start | bytes 24584 | tf_op jit(solution)/shard_map/ppermute | solution.py:306
  12.1 15.8 %collective-permute-start = (bf16[1,4,3,128]{3,1,2,0:T(4,128)(2,1)S(1)}, bf16[1,4,3,128]{3,1,2,0:T(4,128)(2,1)S(1)}, u32[]{:S(2)}, u32[]{:S(2)}) collective-permute-start(bf16[1,4,3,128]{3,1,2,0:T(4,128)(2,1)S(1)} %get-tuple-element.35), channel_id=1, source_target_pairs={{0,64},{64,128},{128,192},{192,0},{1,65},{65,129},{129,193},{193,1... | collective-permute-start | bytes 9224 | tf_op jit(solution)/shard_map/ppermute | solution.py:309
  13.1 14.8 %collective-permute-start.1 = (bf16[1,4,3,128]{3,1,2,0:T(4,128)(2,1)S(1)}, bf16[1,4,3,128]{3,1,2,0:T(4,128)(2,1)S(1)}, u32[]{:S(2)}, u32[]{:S(2)}) collective-permute-start(bf16[1,4,3,128]{3,1,2,0:T(4,128)(2,1)S(1)} %get-tuple-element.36), channel_id=1, source_target_pairs={{0,192},{64,0},{128,64},{192,128},{1,193},{65,1},{129,65},{193,129... | collective-permute-start | bytes 9224 | tf_op jit(solution)/shard_map/ppermute | solution.py:310
  15.9 74.9 %collective-permute-start.24 = (bf16[8,128,256]{2,1,0:T(8,128)(2,1)}, bf16[8,128,256]{2,1,0:T(8,128)(2,1)S(1)}, u32[]{:S(2)}, u32[]{:S(2)}) collective-permute-start(bf16[8,128,256]{2,1,0:T(8,128)(2,1)} %bitcast.96), channel_id=1, source_target_pairs={{0,1},{1,0},{2,3},{3,2},{4,5},{5,4},{6,7},{7,6},{8,9},{9,8},{10,11... | collective-permute-start | bytes 1572872 | tf_op jit(solution)/shard_map/ppermute | solution.py:305
  31.7 76.2 %collective-permute-start.22 = (bf16[8,128,256]{2,1,0:T(8,128)(2,1)S(1)}, bf16[8,128,256]{2,1,0:T(8,128)(2,1)S(1)}, u32[]{:S(2)}, u32[]{:S(2)}) collective-permute-start(bf16[8,128,256]{2,1,0:T(8,128)(2,1)S(1)} %bitcast.100), channel_id=1, source_target_pairs={{0,15},{1,2},{2,1},{3,4},{4,3},{5,6},{6,5},{7,8},{8,7},{9,10},{10,... | collective-permute-start | bytes 1572872 | tf_op jit(solution)/shard_map/ppermute | solution.py:307
  33.1 22.1 %collective-permute-start.4 = (bf16[256,256]{1,0:T(8,128)(2,1)S(1)}, bf16[256,256]{1,0:T(8,128)(2,1)S(1)}, u32[]{:S(2)}, u32[]{:S(2)}) collective-permute-start(bf16[256,256]{1,0:T(8,128)(2,1)S(1)} %get-tuple-element.19), channel_id=1, source_target_pairs={{0,16},{16,32},{32,48},{48,0},{1,17},{17,33},{33,49},{49,1},{2,18}... | collective-permute-start | bytes 393224 | tf_op jit(solution)/shard_map/ppermute | solution.py:368
  51.3 7.2 %collective-permute-start.5 = (bf16[256,256]{1,0:T(8,128)(2,1)S(1)}, bf16[256,256]{1,0:T(8,128)(2,1)S(1)}, u32[]{:S(2)}, u32[]{:S(2)}) collective-permute-start(bf16[256,256]{1,0:T(8,128)(2,1)S(1)} %get-tuple-element.21), channel_id=1, source_target_pairs={{0,32},{16,48},{32,0},{48,16},{1,33},{17,49},{33,1},{49,17},{2,34}... | collective-permute-start | bytes 393224 | tf_op jit(solution)/shard_map/ppermute | solution.py:368
  52.8 7.1 %collective-permute-start.6 = (bf16[256,256]{1,0:T(8,128)(2,1)S(1)}, bf16[256,256]{1,0:T(8,128)(2,1)S(1)}, u32[]{:S(2)}, u32[]{:S(2)}) collective-permute-start(bf16[256,256]{1,0:T(8,128)(2,1)S(1)} %get-tuple-element.20), channel_id=1, source_target_pairs={{0,48},{16,0},{32,16},{48,32},{1,49},{17,1},{33,17},{49,33},{2,50}... | collective-permute-start | bytes 393224 | tf_op jit(solution)/shard_map/ppermute | solution.py:368
  60.8 5.9 %collective-permute-start.7 = (bf16[64,256]{1,0:T(8,128)(2,1)S(1)}, bf16[64,256]{1,0:T(8,128)(2,1)S(1)}, u32[]{:S(2)}, u32[]{:S(2)}) collective-permute-start(bf16[64,256]{1,0:T(8,128)(2,1)S(1)} %get-tuple-element.22), channel_id=1, source_target_pairs={{0,64},{64,128},{128,192},{192,0},{1,65},{65,129},{129,193},{193,1... | collective-permute-start | bytes 98312 | tf_op jit(solution)/shard_map/ppermute | solution.py:372
  60.9 5.8 %collective-permute-start.8 = (bf16[64,256]{1,0:T(8,128)(2,1)S(1)}, bf16[64,256]{1,0:T(8,128)(2,1)S(1)}, u32[]{:S(2)}, u32[]{:S(2)}) collective-permute-start(bf16[64,256]{1,0:T(8,128)(2,1)S(1)} %get-tuple-element.24), channel_id=1, source_target_pairs={{0,128},{64,192},{128,0},{192,64},{1,129},{65,193},{129,1},{193,65... | collective-permute-start | bytes 98312 | tf_op jit(solution)/shard_map/ppermute | solution.py:372
  73.7 7.2 %collective-permute-start.13 = (bf16[64,256]{1,0:T(8,128)(2,1)S(1)}, bf16[64,256]{1,0:T(8,128)(2,1)S(1)}, u32[]{:S(2)}, u32[]{:S(2)}) collective-permute-start(bf16[64,256]{1,0:T(8,128)(2,1)S(1)} %get-tuple-element.5), channel_id=1, source_target_pairs={{0,1},{1,0},{2,3},{3,2},{4,5},{5,4},{6,7},{7,6},{8,9},{9,8},{10,11... | collective-permute-start | bytes 98312 | tf_op jit(solution)/shard_map/ppermute | solution.py:379
  73.8 7.9 %collective-permute-start.14 = (bf16[64,256]{1,0:T(8,128)(2,1)S(1)}, bf16[64,256]{1,0:T(8,128)(2,1)S(1)}, u32[]{:S(2)}, u32[]{:S(2)}) collective-permute-start(bf16[64,256]{1,0:T(8,128)(2,1)S(1)} %get-tuple-element.5), channel_id=1, source_target_pairs={{0,2},{1,3},{2,0},{3,1},{4,6},{5,7},{6,4},{7,5},{8,10},{9,11},{10,... | collective-permute-start | bytes 98312 | tf_op jit(solution)/shard_map/ppermute | solution.py:379
  78.9 7.3 %collective-permute-start.15 = (bf16[64,256]{1,0:T(8,128)(2,1)S(1)}, bf16[64,256]{1,0:T(8,128)(2,1)S(1)}, u32[]{:S(2)}, u32[]{:S(2)}) collective-permute-start(bf16[64,256]{1,0:T(8,128)(2,1)S(1)} %get-tuple-element.5), channel_id=1, source_target_pairs={{0,3},{1,2},{2,1},{3,0},{4,7},{5,6},{6,5},{7,4},{8,11},{9,10},{10,... | collective-permute-start | bytes 98312 | tf_op jit(solution)/shard_map/ppermute | solution.py:379
  86.5 52.8 %collective-permute-start.16 = (bf16[2,32,256]{2,1,0:T(8,128)(2,1)S(1)}, bf16[2,32,256]{2,1,0:T(8,128)(2,1)S(1)}, u32[]{:S(2)}, u32[]{:S(2)}) collective-permute-start(bf16[2,32,256]{2,1,0:T(8,128)(2,1)S(1)} %multiply_convert_fusion), channel_id=1, source_target_pairs={{0,64},{64,128},{128,192},{192,0},{1,65},{65,129},{129,193},{193,1... | collective-permute-start | bytes 98312 | tf_op jit(solution)/shard_map/ppermute | solution.py:392
  88.4 50.9 %collective-permute-start.17 = (bf16[2,32,256]{2,1,0:T(8,128)(2,1)S(1)}, bf16[2,32,256]{2,1,0:T(8,128)(2,1)S(1)}, u32[]{:S(2)}, u32[]{:S(2)}) collective-permute-start(bf16[2,32,256]{2,1,0:T(8,128)(2,1)S(1)} %multiply_convert_fusion), channel_id=1, source_target_pairs={{0,128},{64,192},{128,0},{192,64},{1,129},{65,193},{129,1},{193,65... | collective-permute-start | bytes 98312 | tf_op jit(solution)/shard_map/ppermute | solution.py:392
  90.2 49.1 %collective-permute-start.18 = (bf16[2,32,256]{2,1,0:T(8,128)(2,1)S(1)}, bf16[2,32,256]{2,1,0:T(8,128)(2,1)S(1)}, u32[]{:S(2)}, u32[]{:S(2)}) collective-permute-start(bf16[2,32,256]{2,1,0:T(8,128)(2,1)S(1)} %multiply_convert_fusion), channel_id=1, source_target_pairs={{0,192},{64,0},{128,64},{192,128},{1,193},{65,1},{129,65},{193,129... | collective-permute-start | bytes 98312 | tf_op jit(solution)/shard_map/ppermute | solution.py:392
  127.1 7.9 %collective-permute-start.26 = (bf16[4,128,256]{2,1,0:T(8,128)(2,1)S(1)}, bf16[4,128,256]{2,1,0:T(8,128)(2,1)S(1)}, u32[]{:S(2)}, u32[]{:S(2)}) collective-permute-start(bf16[4,128,256]{2,1,0:T(8,128)(2,1)S(1)} %get-tuple-element.18), channel_id=1, source_target_pairs={{0,16},{16,32},{32,48},{48,0},{1,17},{17,33},{33,49},{49,1},{2,18}... | collective-permute-start | bytes 786440 | tf_op jit(solution)/shard_map/ppermute | solution.py:400
  127.4 8.4 %collective-permute-start.27 = (bf16[4,128,256]{2,1,0:T(8,128)(2,1)S(1)}, bf16[4,128,256]{2,1,0:T(8,128)(2,1)S(1)}, u32[]{:S(2)}, u32[]{:S(2)}) collective-permute-start(bf16[4,128,256]{2,1,0:T(8,128)(2,1)S(1)} %get-tuple-element.17), channel_id=1, source_target_pairs={{0,48},{16,0},{32,16},{48,32},{1,49},{17,1},{33,17},{49,33},{2,50}... | collective-permute-start | bytes 786440 | tf_op jit(solution)/shard_map/ppermute | solution.py:399
  137.1 15.3 %collective-permute-start.29 = (bf16[4,128,256]{2,1,0:T(8,128)(2,1)S(1)}, bf16[4,128,256]{2,1,0:T(8,128)(2,1)S(1)}, u32[]{:S(2)}, u32[]{:S(2)}) collective-permute-start(bf16[4,128,256]{2,1,0:T(8,128)(2,1)S(1)} %pad_maximum_fusion.1), channel_id=1, source_target_pairs={{0,192},{64,0},{128,64},{192,128},{1,193},{65,1},{129,65},{193,129... | collective-permute-start | bytes 786440 | tf_op jit(solution)/shard_map/ppermute | solution.py:407
  138.8 13.6 %collective-permute-start.28 = (bf16[4,128,256]{2,1,0:T(8,128)(2,1)S(1)}, bf16[4,128,256]{2,1,0:T(8,128)(2,1)S(1)}, u32[]{:S(2)}, u32[]{:S(2)}) collective-permute-start(bf16[4,128,256]{2,1,0:T(8,128)(2,1)S(1)} %pad_maximum_fusion), channel_id=1, source_target_pairs={{0,64},{64,128},{128,192},{192,0},{1,65},{65,129},{129,193},{193,1... | collective-permute-start | bytes 786440 | tf_op jit(solution)/shard_map/ppermute | solution.py:408
  139.3 13.0 %collective-permute-start.19 = (bf16[256,256]{1,0:T(8,128)(2,1)S(1)}, bf16[256,256]{1,0:T(8,128)(2,1)S(1)}, u32[]{:S(2)}, u32[]{:S(2)}) collective-permute-start(bf16[256,256]{1,0:T(8,128)(2,1)S(1)} %bitcast.104), channel_id=1, source_target_pairs={{0,16},{16,32},{32,48},{48,0},{1,17},{17,33},{33,49},{49,1},{2,18}... | collective-permute-start | bytes 393224 | tf_op jit(solution)/shard_map/ppermute | solution.py:394
  141.2 11.2 %collective-permute-start.20 = (bf16[256,256]{1,0:T(8,128)(2,1)S(1)}, bf16[256,256]{1,0:T(8,128)(2,1)S(1)}, u32[]{:S(2)}, u32[]{:S(2)}) collective-permute-start(bf16[256,256]{1,0:T(8,128)(2,1)S(1)} %bitcast.105), channel_id=1, source_target_pairs={{0,32},{16,48},{32,0},{48,16},{1,33},{17,49},{33,1},{49,17},{2,34}... | collective-permute-start | bytes 393224 | tf_op jit(solution)/shard_map/ppermute | solution.py:394
  142.5 9.9 %collective-permute-start.21 = (bf16[256,256]{1,0:T(8,128)(2,1)S(1)}, bf16[256,256]{1,0:T(8,128)(2,1)S(1)}, u32[]{:S(2)}, u32[]{:S(2)}) collective-permute-start(bf16[256,256]{1,0:T(8,128)(2,1)S(1)} %bitcast.106), channel_id=1, source_target_pairs={{0,48},{16,0},{32,16},{48,32},{1,49},{17,1},{33,17},{49,33},{2,50}... | collective-permute-start | bytes 393224 | tf_op jit(solution)/shard_map/ppermute | solution.py:394
  (21 other events, 281.3 us)
